TPU v7x, 32 devices: a whole 2x2x4 slice. The times are simulated.
32 devices in a mesh: batch: 4 (over x, core), blk: 8 (over z, y).
Axes of the slice: x: 2, y: 2, z: 4, core: 2. Of those that a mesh axis runs over, the one named last changes fastest.
Arguments:
- inputs: bfloat16 [32, 1024, 768], P('batch', 'blk'), may hold values from -6 to 6
- cotangent: bfloat16 [32, 1024, 768], P('batch', 'blk'), may hold values from -6 to 6
- group_counts: int32 [4], replicated, may hold values from 1 to 8, as said below
- first_gain: float32 [768], replicated, may hold values from 0.5 to 1.5
- first_bias: float32 [768], replicated, may hold values from -1.25 to 1.25
- qkv_weight: bfloat16 [768, 2304], replicated, may hold values from -0.21875 to 0.21875
- qkv_bias: float32 [2304], replicated, may hold values from -1.25 to 1.25
- out_weight: bfloat16 [768, 768], replicated, may hold values from -1.75 to 1.75
- out_bias: float32 [768], replicated, may hold values from -1.25 to 1.25
- second_gain: float32 [768], replicated, may hold values from 0.5 to 1.5
- second_bias: float32 [768], replicated, may hold values from -1.25 to 1.25
- up_weight: bfloat16 [768, 3072], replicated, may hold values from -0.21875 to 0.21875
- up_bias: float32 [3072], replicated, may hold values from -1.25 to 1.25
- down_weight: bfloat16 [3072, 768], replicated, may hold values from -0.109375 to 0.109375
- down_bias: float32 [768], replicated, may hold values from -1.25 to 1.25
- compress: bfloat16 [256, 1024], P(None, 'blk'), may hold values from -0.1875 to 0.1875
Outputs:
- output: bfloat16 [32, 1024, 768], P('batch', 'blk')
- input_grad: bfloat16 [32, 1024, 768], P('batch', 'blk')
- first_gain_grad: float32 [768], P('blk')
- first_bias_grad: float32 [768], P('blk')
- qkv_weight_grad: float32 [768, 2304], P('blk')
- qkv_bias_grad: float32 [2304], P('blk')
- out_weight_grad: float32 [768, 768], P('blk')
- out_bias_grad: float32 [768], P('blk')
- second_gain_grad: float32 [768], P('blk')
- second_bias_grad: float32 [768], P('blk')
- up_weight_grad: float32 [768, 3072], P('blk')
- up_bias_grad: float32 [3072], P('blk')
- down_weight_grad: float32 [3072, 768], P('blk')
- down_bias_grad: float32 [768], P('blk')
- compress_grad: float32 [256, 1024], P(None, 'blk')
Inputs may be any that keep to these rules, and one draw needn't show every extreme that they name: Group g holds sequences in its slots 0 to group_counts[g] - 1; the counts of all groups add up to exactly 20; in every draw some group uses all 8 slots and some group uses one.
All inputs are finite; a program needn't handle non-finite values.
Results may differ from a plain program's by a relative error of at most 0.02.
Values may be sent and summed in bfloat16 or wider, within the bound.
A program may use at most 192 MiB of HBM per device.

v0:
```python
import math
import jax
import jax.numpy as jnp
from jax import lax
from jax.sharding import PartitionSpec as P

H = 12
HD = 64


def layer_norm(states, factor, offset):
    center = states - jnp.mean(states, axis=-1, keepdims=True)
    spread = jnp.mean(center * center, axis=-1, keepdims=True)
    return center * lax.rsqrt(spread + 1e-05) * factor + offset


def gelu_tanh(values):
    return jax.nn.gelu(values, approximate=True)


def run_layer(
    inputs,
    cotangent,
    alive,
    first_gain,
    first_bias,
    qkv_weight,
    qkv_bias,
    out_weight,
    out_bias,
    second_gain,
    second_bias,
    up_weight,
    up_bias,
    down_weight,
    down_bias,
    compress,
):
    slots, tokens, width = inputs.shape
    rows = slots * tokens
    summary_len = compress.shape[0]
    factor = 1.0 / math.sqrt(HD)
    states = inputs.astype(jnp.float32)
    normed_first, first_back = jax.vjp(layer_norm, states, first_gain, first_bias)
    first_low = normed_first.astype(jnp.bfloat16).reshape(rows, width)
    project = jnp.dot(first_low, qkv_weight, preferred_element_type=jnp.float32) + qkv_bias
    query_low = project[:, :width].astype(jnp.bfloat16).reshape(slots, tokens, H, HD)
    pair_low = project[:, width:].astype(jnp.bfloat16).reshape(slots, tokens, 2 * width)
    partial_summary = jnp.einsum(
        "jt,stc->sjc", compress, pair_low, preferred_element_type=jnp.float32
    )
    summary_low = lax.psum(partial_summary, "blk").astype(jnp.bfloat16)
    key_low = summary_low[..., :width].reshape(slots, summary_len, H, HD)
    value_low = summary_low[..., width:].reshape(slots, summary_len, H, HD)
    scores = (
        jnp.einsum("sthd,sjhd->shtj", query_low, key_low, preferred_element_type=jnp.float32)
        * factor
    )
    highest = jnp.max(scores, axis=-1, keepdims=True)
    expo = jnp.exp(scores - highest)
    totals = jnp.sum(expo, axis=-1, keepdims=True)
    logsum = highest + jnp.log(totals)
    weights_low = (expo / totals).astype(jnp.bfloat16)
    mixed = jnp.einsum(
        "shtj,sjhd->sthd", weights_low, value_low, preferred_element_type=jnp.float32
    )
    mixed_low = mixed.reshape(rows, width).astype(jnp.bfloat16)
    branch = jnp.dot(mixed_low, out_weight, preferred_element_type=jnp.float32) + out_bias
    middle = states + branch.reshape(slots, tokens, width)
    second_normed, second_back = jax.vjp(layer_norm, middle, second_gain, second_bias)
    second_low = second_normed.astype(jnp.bfloat16).reshape(rows, width)
    hidden = jnp.dot(second_low, up_weight, preferred_element_type=jnp.float32) + up_bias
    active, gelu_back = jax.vjp(gelu_tanh, hidden)
    active_low = active.astype(jnp.bfloat16)
    result = middle + (
        jnp.dot(active_low, down_weight, preferred_element_type=jnp.float32) + down_bias
    ).reshape(slots, tokens, width)
    output = jnp.where(alive, result, 0.0).astype(jnp.bfloat16)
    incoming = jnp.where(alive, cotangent, jnp.zeros_like(cotangent)).reshape(rows, width)
    incoming_full = incoming.astype(jnp.float32)
    down_grad = jnp.einsum("rf,rd->fd", active_low, incoming, preferred_element_type=jnp.float32)
    down_bias_grad = jnp.sum(incoming_full, axis=0)
    active_grad = jnp.einsum("rd,fd->rf", incoming, down_weight, preferred_element_type=jnp.float32)
    hidden_low = gelu_back(active_grad)[0].astype(jnp.bfloat16)
    up_grad = jnp.einsum("rd,rf->df", second_low, hidden_low, preferred_element_type=jnp.float32)
    up_bias_grad = jnp.sum(hidden_low.astype(jnp.float32), axis=0)
    second_grad = jnp.einsum("rf,df->rd", hidden_low, up_weight, preferred_element_type=jnp.float32)
    middle_part, second_gain_grad, second_bias_grad = second_back(
        second_grad.reshape(slots, tokens, width)
    )
    middle_grad = incoming_full.reshape(slots, tokens, width) + middle_part
    branch_low = middle_grad.reshape(rows, width).astype(jnp.bfloat16)
    out_grad = jnp.einsum("rd,re->de", mixed_low, branch_low, preferred_element_type=jnp.float32)
    out_bias_grad = jnp.sum(branch_low.astype(jnp.float32), axis=0)
    mixed_grad = jnp.einsum("re,de->rd", branch_low, out_weight, preferred_element_type=jnp.float32)
    mixed_grad_low = mixed_grad.astype(jnp.bfloat16).reshape(slots, tokens, H, HD)
    scores_again = (
        jnp.einsum("sthd,sjhd->shtj", query_low, key_low, preferred_element_type=jnp.float32)
        * factor
    )
    weights_again = jnp.exp(scores_again - logsum)
    weights_again_low = weights_again.astype(jnp.bfloat16)
    weight_grad = jnp.einsum(
        "sthd,sjhd->shtj", mixed_grad_low, value_low, preferred_element_type=jnp.float32
    )
    value_summary_grad = jnp.einsum(
        "shtj,sthd->sjhd", weights_again_low, mixed_grad_low, preferred_element_type=jnp.float32
    )
    inner = jnp.sum(weights_again * weight_grad, axis=-1, keepdims=True)
    score_low = (weights_again * (weight_grad - inner)).astype(jnp.bfloat16)
    query_grad = (
        jnp.einsum("shtj,sjhd->sthd", score_low, key_low, preferred_element_type=jnp.float32)
        * factor
    )
    key_summary_grad = (
        jnp.einsum("shtj,sthd->sjhd", score_low, query_low, preferred_element_type=jnp.float32)
        * factor
    )
    summary_grad = jnp.concatenate(
        [
            key_summary_grad.reshape(slots, summary_len, width),
            value_summary_grad.reshape(slots, summary_len, width),
        ],
        axis=-1,
    )
    summary_grad_low = lax.psum(summary_grad.astype(jnp.bfloat16), "blk")
    pair_grad = jnp.einsum(
        "jt,sjc->stc", compress, summary_grad_low, preferred_element_type=jnp.float32
    )
    compress_grad = jnp.einsum(
        "sjc,stc->jt", summary_grad_low, pair_low, preferred_element_type=jnp.float32
    )
    project_low = jnp.concatenate(
        [query_grad.reshape(rows, width), pair_grad.reshape(rows, 2 * width)], axis=-1
    ).astype(jnp.bfloat16)
    qkv_grad = jnp.einsum("rd,rc->dc", first_low, project_low, preferred_element_type=jnp.float32)
    qkv_bias_grad = jnp.sum(project_low.astype(jnp.float32), axis=0)
    first_grad = jnp.einsum(
        "rc,dc->rd", project_low, qkv_weight, preferred_element_type=jnp.float32
    )
    state_part, first_gain_grad, first_bias_grad = first_back(
        first_grad.reshape(slots, tokens, width)
    )
    input_grad = (middle_grad + state_part).astype(jnp.bfloat16)
    grads = (
        first_gain_grad,
        first_bias_grad,
        qkv_grad,
        qkv_bias_grad,
        out_grad,
        out_bias_grad,
        second_gain_grad,
        second_bias_grad,
        up_grad,
        up_bias_grad,
        down_grad,
        down_bias_grad,
    )
    return (output, input_grad, grads, compress_grad)


def body(
    inputs,
    cotangent,
    group_counts,
    first_gain,
    first_bias,
    qkv_weight,
    qkv_bias,
    out_weight,
    out_bias,
    second_gain,
    second_bias,
    up_weight,
    up_bias,
    down_weight,
    down_bias,
    compress,
):
    slots = inputs.shape[0]
    weights_all = (
        first_gain,
        first_bias,
        qkv_weight,
        qkv_bias,
        out_weight,
        out_bias,
        second_gain,
        second_bias,
        up_weight,
        up_bias,
        down_weight,
        down_bias,
        compress,
    )
    group_index = lax.axis_index("batch")
    my_count = group_counts[group_index]
    alive = (jnp.arange(slots, dtype=jnp.int32) < my_count)[:, None, None]
    output, input_grad, grads, compress_grad = run_layer(inputs, cotangent, alive, *weights_all)
    (
        first_gain_grad,
        first_bias_grad,
        qkv_grad,
        qkv_bias_grad,
        out_grad,
        out_bias_grad,
        second_gain_grad,
        second_bias_grad,
        up_grad,
        up_bias_grad,
        down_grad,
        down_bias_grad,
    ) = grads
    (
        first_gain_rows,
        first_bias_rows,
        qkv_rows,
        qkv_bias_rows,
        out_rows,
        out_bias_rows,
        second_gain_rows,
        second_bias_rows,
        up_rows,
        up_bias_rows,
        down_rows,
        down_bias_rows,
    ) = (
        lax.psum_scatter(
            first_gain_grad.astype(jnp.bfloat16), "blk", scatter_dimension=0, tiled=True
        ).astype(jnp.float32),
        lax.psum_scatter(
            first_bias_grad.astype(jnp.bfloat16), "blk", scatter_dimension=0, tiled=True
        ).astype(jnp.float32),
        lax.psum_scatter(
            qkv_grad.astype(jnp.bfloat16), "blk", scatter_dimension=0, tiled=True
        ).astype(jnp.float32),
        lax.psum_scatter(
            qkv_bias_grad.astype(jnp.bfloat16), "blk", scatter_dimension=0, tiled=True
        ).astype(jnp.float32),
        lax.psum_scatter(
            out_grad.astype(jnp.bfloat16), "blk", scatter_dimension=0, tiled=True
        ).astype(jnp.float32),
        lax.psum_scatter(
            out_bias_grad.astype(jnp.bfloat16), "blk", scatter_dimension=0, tiled=True
        ).astype(jnp.float32),
        lax.psum_scatter(
            second_gain_grad.astype(jnp.bfloat16), "blk", scatter_dimension=0, tiled=True
        ).astype(jnp.float32),
        lax.psum_scatter(
            second_bias_grad.astype(jnp.bfloat16), "blk", scatter_dimension=0, tiled=True
        ).astype(jnp.float32),
        lax.psum_scatter(
            up_grad.astype(jnp.bfloat16), "blk", scatter_dimension=0, tiled=True
        ).astype(jnp.float32),
        lax.psum_scatter(
            up_bias_grad.astype(jnp.bfloat16), "blk", scatter_dimension=0, tiled=True
        ).astype(jnp.float32),
        lax.psum_scatter(
            down_grad.astype(jnp.bfloat16), "blk", scatter_dimension=0, tiled=True
        ).astype(jnp.float32),
        lax.psum_scatter(
            down_bias_grad.astype(jnp.bfloat16), "blk", scatter_dimension=0, tiled=True
        ).astype(jnp.float32),
    )
    summed = (
        lax.psum(first_gain_rows.astype(jnp.bfloat16), "batch").astype(jnp.float32),
        lax.psum(first_bias_rows.astype(jnp.bfloat16), "batch").astype(jnp.float32),
        lax.psum(qkv_rows.astype(jnp.bfloat16), "batch").astype(jnp.float32),
        lax.psum(qkv_bias_rows.astype(jnp.bfloat16), "batch").astype(jnp.float32),
        lax.psum(out_rows.astype(jnp.bfloat16), "batch").astype(jnp.float32),
        lax.psum(out_bias_rows.astype(jnp.bfloat16), "batch").astype(jnp.float32),
        lax.psum(second_gain_rows.astype(jnp.bfloat16), "batch").astype(jnp.float32),
        lax.psum(second_bias_rows.astype(jnp.bfloat16), "batch").astype(jnp.float32),
        lax.psum(up_rows.astype(jnp.bfloat16), "batch").astype(jnp.float32),
        lax.psum(up_bias_rows.astype(jnp.bfloat16), "batch").astype(jnp.float32),
        lax.psum(down_rows.astype(jnp.bfloat16), "batch").astype(jnp.float32),
        lax.psum(down_bias_rows.astype(jnp.bfloat16), "batch").astype(jnp.float32),
        lax.psum(compress_grad.astype(jnp.bfloat16), "batch").astype(jnp.float32),
    )
    return (output, input_grad) + tuple(summed)


def solution(mesh):
    placed = (
        P("batch", "blk", None),
        P("batch", "blk", None),
        P(),
        P(),
        P(),
        P(),
        P(),
        P(),
        P(),
        P(),
        P(),
        P(),
        P(),
        P(),
        P(),
        P(None, "blk"),
    )
    return jax.shard_map(
        body,
        mesh=mesh,
        in_specs=placed,
        out_specs=(
            P("batch", "blk", None),
            P("batch", "blk", None),
            P("blk"),
            P("blk"),
            P("blk", None),
            P("blk"),
            P("blk", None),
            P("blk"),
            P("blk"),
            P("blk"),
            P("blk", None),
            P("blk"),
            P("blk", None),
            P("blk"),
            P(None, "blk"),
        ),
        check_vma=False,
    )
```

profile of v0, /device:TPU:0, one launch (start us, length us, event | category | flops | bytes accessed | tf_op | source)
XLA Modules:
  0.0 1306.0 jit_solution(606664537931861903)
XLA Ops:
  9.1 2.1 fusion.23
  12.6 4.1 add_convert_fusion
  21.0 2.6 copy.53
  23.6 3.2 copy.68
  26.8 7.2 convolution_bitcast_fusion
  34.0 487.1 %all-reduce.18 = bf16[8,256,1536]{1,2,0:T(8,128)(2,1)} all-reduce(f32[8,256,1536]{1,2,0:T(8,128)} %convolution_bitcast_fusion), channel_id=1, replica_groups=mesh['batch'=4,'blk'=8] {'blk'}, use_global_device_ids=true, to_apply=%region_2.0 | all-reduce | flops 3145728 | bytes 18874368 | tf_op jit(solution)/shard_map/psum | solution.py:52
  521.0 3.5 fusion.62
  524.6 2.7 multiply_reduce_fusion.1
  527.3 3.7 fusion.7
  532.1 6.3 fusion.36
  546.4 8.0 fusion.66
  554.4 11.1 convolution_add_fusion.1
  565.5 16.9 %fusion.65 = (bf16[3072]{0:T(1024)(128)(2,1)}, bf16[1024,3072]{1,0:T(8,128)(2,1)}) fusion(f32[1024,3072]{1,0:T(8,128)} %fusion.66, f32[3072]{0:T(1024)S(1)} %copy-done.40, bf16[1024,768]{1,0:T(8,128)(2,1)S(1)} %bitcast.116, bf16[3072,768]{1,0:T(8,128)(2,1)S(1)} %bitcast.135), kind=kOutput, calls=%fused_computation.106 | convolution fusion | flops 4901041152 | bytes 25184256 | tf_op jit(solution)/shard_map/rd,fd->rf/dot_general | solution.py:83
  582.4 9.2 fusion.64
  593.3 3.1 add_add_fusion.1
  596.4 2.1 reduce_sum.212
  598.6 3.6 fusion.59
  603.3 2.6 convolution_convert_fusion.4
  605.9 2.6 copy.56
  608.5 1.9 copy.70
  610.4 7.3 fusion.25
  617.7 13.5 %multiply_reduce_fusion = (f32[8,12,128]{2,1,0:T(8,128)}, f32[8,12,128,256]{3,2,1,0:T(8,128)}) fusion(f32[8,12,128,256]{3,2,1,0:T(8,128)} %copy-done.1, f32[8,12,128]{2,1,0:T(8,128)S(1)} %copy-done.23, bf16[8,256,12,64]{1,3,2,0:T(8,128)(2,1)S(1)} %bitcast.119, bf16[8,128,12,64]{1,0,3,2:T(8,128)(2,1)S(1)} %bitcast.112), kind=kOutput, calls=%fused_computation.10 | convolution fusion | flops 415223808 | bytes 29982720 | tf_op jit(solution)/shard_map/sthd,sjhd->shtj/dot_general | solution.py:103
  631.1 4.7 copy.62
  635.8 10.4 multiply_convert_fusion
  646.2 3.1 multiply_convert_fusion.2
  649.8 4.7 copy.61
  654.5 6.0 pad_maximum_fusion
  660.6 4.3 fusion.33
  664.9 12.8 convolution_convert_fusion
  677.8 9.2 convolution_convert_fusion.1
  687.0 6.1 fusion.37
  696.0 2.8 copy.64
  698.8 171.5 %all-reduce.15.cloned.1.call-done = bf16[8,256,1536]{2,1,0:T(8,128)(2,1)} async-done(((bf16[8,256,1536]{2,1,0:T(8,128)(2,1)}), bf16[8,256,1536]{2,1,0:T(8,128)(2,1)}) %all-reduce.15.cloned.1.call-update) | async-done | bytes 6291472 | tf_op jit(solution)/shard_map/psum | solution.py:126
  870.2 4.0 convolution_convert_fusion.3
  875.9 5.4 convolution_convert_fusion.2
  884.5 6.4 fusion.63
  891.8 2.2 fusion.22
  895.9 2.4 fusion.49
  898.3 39.3 %reduce-scatter.7.cloned.1.call-done = bf16[96,768]{1,0:T(8,128)(2,1)} async-done(((bf16[768,768]{1,0:T(8,128)(2,1)}), bf16[96,768]{1,0:T(8,128)(2,1)}) %reduce-scatter.7.cloned.1.call-update) | async-done | bytes 147472 | tf_op jit(solution)/shard_map/reduce_scatter | solution.py:240
  937.7 98.3 %reduce-scatter.11.cloned.1.call-done = bf16[384,768]{1,0:T(8,128)(2,1)} async-done(((bf16[3072,768]{1,0:T(8,128)(2,1)}), bf16[384,768]{1,0:T(8,128)(2,1)}) %reduce-scatter.11.cloned.1.call-update) | async-done | bytes 589840 | tf_op jit(solution)/shard_map/reduce_scatter | solution.py:258
  1036.0 99.0 %reduce-scatter.9.cloned.1.call-done = bf16[96,3072]{1,0:T(8,128)(2,1)} async-done(((bf16[768,3072]{1,0:T(8,128)(2,1)}), bf16[96,3072]{1,0:T(8,128)(2,1)}) %reduce-scatter.9.cloned.1.call-update) | async-done | bytes 589840 | tf_op jit(solution)/shard_map/reduce_scatter | solution.py:252
  1135.0 82.6 %reduce-scatter.5.cloned.1.call-done = bf16[96,2304]{1,0:T(8,128)(2,1)} async-done(((bf16[768,2304]{1,0:T(8,128)(2,1)}), bf16[96,2304]{1,0:T(8,128)(2,1)}) %reduce-scatter.5.cloned.1.call-update) | async-done | bytes 442384 | tf_op jit(solution)/shard_map/reduce_scatter | solution.py:234
  1217.6 3.7 fusion.46
  1221.2 37.0 %all-reduce.8 = (bf16[768]{0:T(1024)(128)(2,1)}, bf16[768]{0:T(1024)(128)(2,1)}, bf16[2304]{0:T(1024)(128)(2,1)}, bf16[768]{0:T(1024)(128)(2,1)}, bf16[768]{0:T(...) all-reduce(bf16[768]{0:T(1024)(128)(2,1)} %get-tuple-element.17, ...), channel_id=2, replica_groups=mesh['batch'=4,'blk'=8] {'blk'}, use_global_device_ids=true, to_apply=%region_14.15.clone | all-reduce | flops 9984 | bytes 39936
  1268.5 6.4 all-reduce.9
  1285.1 5.4 add_convert_fusion.1
  1293.7 2.0 convert_element_type.183
  1295.6 2.2 convert_element_type.193
  (163 shorter events, 53.2 us)
Async XLA Ops:
  7.2 5.4 copy-start
  7.2 4.6 copy-start.29
  7.2 4.6 copy-start.35
  7.2 863.0 %all-reduce.15.cloned.1.call-start = ((), (), s32[]{:S(2)}) async-start(), calls=%async_computation.4 | async-start | bytes 12582912 | tf_op jit(solution)/shard_map/psum | solution.py:126
  7.3 4.6 copy-start.2
  7.3 5.3 copy-start.39
  9.1 3.4 copy-start.25
  12.5 4.1 copy-start.18
  17.9 1.9 copy-start.43
  23.6 3.2 copy-start.7
  521.0 3.5 copy-start.11
  524.5 2.8 copy-start.9
  524.5 7.5 copy-start.14
  527.3 4.8 copy-start.1
  539.7 1.5 copy-start.20
  539.7 2.0 copy-start.3
  542.0 1.4 copy-start.17
  542.1 2.6 copy-start.31
  542.1 2.6 copy-start.36
  542.1 4.3 slice-start.4
  543.4 3.0 slice-start.5
  544.6 20.9 %copy-start.13 = (bf16[8,128,768]{2,1,0:T(8,128)(2,1)}, bf16[8,128,768]{2,1,0:T(8,128)(2,1)S(1)}, u32[]{:S(2)}) copy-start(bf16[8,128,768]{2,1,0:T(8,128)(2,1)S(1)} %get-tuple-element.41) | copy-start | bytes 4718596
  544.7 9.7 slice-start.2
  546.4 8.0 slice-start.3
  546.4 8.0 copy-start.40
  546.4 8.0 copy-start.42
  598.6 3.6 copy-start.32
  598.6 4.8 copy-start.38
  608.5 1.9 copy-start.23
  610.4 7.3 copy-start.15
  635.8 10.4 copy-start.12
  646.2 3.6 copy-start.5
  660.5 277.1 %reduce-scatter.7.cloned.1.call-start = ((), (), s32[]{:S(2)}) async-start(), calls=%async_computation.6 | async-start | bytes 1327104 | tf_op jit(solution)/shard_map/reduce_scatter | solution.py:240
  664.9 371.1 %reduce-scatter.11.cloned.1.call-start = ((), (), s32[]{:S(2)}) async-start(), calls=%async_computation.8 | async-start | bytes 5308416 | tf_op jit(solution)/shard_map/reduce_scatter | solution.py:258
  677.7 457.3 %reduce-scatter.9.cloned.1.call-start = ((), (), s32[]{:S(2)}) async-start(), calls=%async_computation.7 | async-start | bytes 5308416 | tf_op jit(solution)/shard_map/reduce_scatter | solution.py:252
  687.0 530.6 %reduce-scatter.5.cloned.1.call-start = ((), (), s32[]{:S(2)}) async-start(), calls=%async_computation.5 | async-start | bytes 3981312 | tf_op jit(solution)/shard_map/reduce_scatter | solution.py:234
  870.2 5.7 copy-start.16
  870.2 5.7 copy-start.19
  874.3 1.6 copy-start.10
  881.3 409.2 %all-reduce.17.cloned.1.call-start = ((), (), s32[]{:S(2)}) async-start(), calls=%async_computation.9 | async-start | bytes 3670016 | tf_op jit(solution)/shard_map/psum | solution.py:268
  884.4 6.5 copy-start.4
  884.4 6.5 copy-start.26
  884.4 6.5 copy-start.30
  890.9 3.1 copy-start.6
  890.9 3.4 slice-start
  891.8 3.3 slice-start.1
  891.8 4.2 copy-start.8
  1290.5 7.4 copy-start.24
  (9 other events, 8.5 us)
Sparse Core Ops, SparseCore 0:
  660.6 209.5 all-reduce.14
  874.6 63.0 reduce-scatter.6
  941.8 94.1 reduce-scatter.10
  1039.9 94.9 reduce-scatter.8
  1138.9 78.6 reduce-scatter.4
  1220.9 47.4 all-reduce.16
where the time goes:
time: 1310 us
  blocking collectives  531 us (41%)
  waiting for transfers between devices  491 us (37%)
  matrix products  144 us (11%)
  other arithmetic  70.1 us (5%)
  local copies, waits for them, and re-layouts  53.4 us (4%)
  between operations  17 us (1%)
    psum x1, blocking collectives, run_layer(): summary_low = lax.psum(partial_summary, 'blk').astype(jnp.bfloat16)  487 us
    psum x1, waiting for transfers between devices, run_layer(): summary_grad_low = lax.psum(summary_grad.astype(jnp.bfloat16), 'blk')  171 us
    reduce_scatter x1, waiting for transfers between devices, body(): lax.psum_scatter(up_grad.astype(jnp.bfloat16), 'blk', scatter_dimension=0...  99 us
    reduce_scatter x1, waiting for transfers between devices, body(): lax.psum_scatter(down_grad.astype(jnp.bfloat16), 'blk', scatter_dimension...  98.3 us
    reduce_scatter x1, waiting for transfers between devices, body(): lax.psum_scatter(qkv_grad.astype(jnp.bfloat16), 'blk', scatter_dimension=...  82.6 us
    reduce_scatter x1, waiting for transfers between devices, body(): lax.psum_scatter(out_grad.astype(jnp.bfloat16), 'blk', scatter_dimension=...  39.3 us
    unnamed x1, blocking collectives  37 us
    unnamed x114, local copies, waits for them, and re-layouts  26.5 us
  transfers between devices with their start and end apart: 6, of which 5 were waited for; matrix products, arithmetic and copies ran while one was open for 7% of the time, Pallas kernels for 0%

commit v1 on v0

--- a/solution.py
+++ b/solution.py
@@ -49,7 +49,7 @@
     partial_summary = jnp.einsum(
         "jt,stc->sjc", compress, pair_low, preferred_element_type=jnp.float32
     )
-    summary_low = lax.psum(partial_summary, "blk").astype(jnp.bfloat16)
+    summary_low = jnp.sum(lax.all_gather(partial_summary, "blk"), axis=0).astype(jnp.bfloat16)
     key_low = summary_low[..., :width].reshape(slots, summary_len, H, HD)
     value_low = summary_low[..., width:].reshape(slots, summary_len, H, HD)
     scores = (

time: 1310 us -> 2780 us (2.12)
  waiting for transfers between devices: 491 us -> 2380 us
  blocking collectives: 531 us -> 43.5 us
  other arithmetic: 70.1 us -> 107 us
  local copies, waits for them, and re-layouts: 53.4 us -> 81.9 us
    all_gather x0 -> x1, waiting for transfers between devices: none -> 1890 us  [run_layer(): lax.all_gather(partial_summary, 'blk')]
    psum x1 -> x0, blocking collectives: 487 us -> none  [run_layer(): summary_low = lax.psum(partial_summary, 'blk').astype(jnp.bfloat16)]
    reduce_sum x0 -> x1, other arithmetic: none -> 34.9 us  [run_layer(): jnp.sum(lax.all_gather(partial_summary, 'blk'), axis=0).astype(jnp.bfloat16)]
  transfers between devices with their start and end apart: 6 -> 7, of which waited for: 5 -> 6; matrix products, arithmetic and copies ran while one was open for 7% -> 4% of each run, Pallas kernels for 0% -> 0%
where the time goes in v1:
time: 2780 us; the launch traced here: 2770 us
  waiting for transfers between devices  2380 us (86%)
  matrix products  143 us (5%)
  other arithmetic  107 us (4%)
  local copies, waits for them, and re-layouts  81.9 us (3%)
  blocking collectives  43.5 us (2%)
    all_gather x1, waiting for transfers between devices, run_layer(): lax.all_gather(partial_summary, 'blk')  1890 us
    psum x1, waiting for transfers between devices, run_layer(): summary_grad_low = lax.psum(summary_grad.astype(jnp.bfloat16), 'blk')  173 us
    reduce_scatter x1, waiting for transfers between devices, body(): lax.psum_scatter(up_grad.astype(jnp.bfloat16), 'blk', scatter_dimension=0...  99 us
    reduce_scatter x1, waiting for transfers between devices, body(): lax.psum_scatter(down_grad.astype(jnp.bfloat16), 'blk', scatter_dimension...  98.2 us
    reduce_scatter x1, waiting for transfers between devices, body(): lax.psum_scatter(qkv_grad.astype(jnp.bfloat16), 'blk', scatter_dimension=...  82.6 us
  transfers between devices with their start and end apart: 7, of which 6 were waited for; matrix products, arithmetic and copies ran while one was open for 4% of the time, Pallas kernels for 0%

profile of v1, /device:TPU:0, one launch (start us, length us, event | category | flops | bytes accessed | tf_op | source)
XLA Modules:
  0.0 2770.4 jit_solution(17559373853912022021)
XLA Ops:
  12.6 4.0 add_convert_fusion
  20.4 6.4 convolution_bitcast_fusion
  26.7 12.6 copy.67
  39.6 2.7 slice.20
  42.2 2.6 copy.69
  44.8 3.0 copy.85
  49.1 3.8 fusion.58
  52.9 1885.4 %all-gather.3.cloned.1.call-done = f32[64,256,1536]{2,1,0:T(8,128)} async-done(((f32[8,256,1536]{2,1,0:T(8,128)}), f32[64,256,1536]{2,1,0:T(8,128)}) %all-gather.3.cloned.1.call-update) | async-done | bytes 100663312 | tf_op jit(solution)/shard_map/all_gather | solution.py:52
  1938.3 34.9 %reduce_sum.217 = bf16[8,256,1536]{2,1,0:T(8,128)(2,1)} reduce(f32[8,8,256,1536]{3,2,1,0:T(8,128)} %bitcast.5, f32[]{:T(128)} %constant.36.clone.1), dimensions={0}, to_apply=%region_2.0 | reduce | flops 22020096 | bytes 106954752 | tf_op jit(solution)/shard_map/reduce_sum | solution.py:52
  1973.2 6.0 fusion.62
  1979.2 4.7 copy.70
  1983.9 4.6 copy.68
  1988.5 5.1 multiply_reduce_fusion.1
  1993.6 3.7 fusion.7
  1998.9 6.6 fusion.36
  2011.8 8.0 fusion.66
  2019.8 11.0 convolution_add_fusion.1
  2030.8 17.2 fusion.65
  2048.0 9.2 fusion.64
  2058.9 2.8 add_add_fusion.1
  2063.8 3.6 fusion.59
  2068.5 2.6 convolution_convert_fusion.4
  2071.1 2.6 copy.73
  2075.7 7.3 fusion.25
  2084.0 9.8 multiply_reduce_fusion
  2093.8 4.6 copy.79
  2098.5 10.4 multiply_convert_fusion
  2108.9 3.0 multiply_convert_fusion.2
  2112.4 4.7 copy.78
  2117.1 6.0 pad_maximum_fusion
  2123.2 4.3 fusion.33
  2127.6 13.3 convolution_convert_fusion
  2141.0 9.2 convolution_convert_fusion.1
  2150.5 6.1 fusion.37
  2159.4 2.6 copy.81
  2162.0 172.5 %all-reduce.14.cloned.1.call-done = bf16[8,256,1536]{2,1,0:T(8,128)(2,1)} async-done(((bf16[8,256,1536]{2,1,0:T(8,128)(2,1)}), bf16[8,256,1536]{2,1,0:T(8,128)(2,1)}) %all-reduce.14.cloned.1.call-update) | async-done | bytes 6291472 | tf_op jit(solution)/shard_map/psum | solution.py:126
  2334.6 4.0 convolution_convert_fusion.3
  2340.2 5.3 convolution_convert_fusion.2
  2348.8 6.4 fusion.63
  2360.2 2.4 fusion.49
  2362.7 39.5 %reduce-scatter.7.cloned.1.call-done = bf16[96,768]{1,0:T(8,128)(2,1)} async-done(((bf16[768,768]{1,0:T(8,128)(2,1)}), bf16[96,768]{1,0:T(8,128)(2,1)}) %reduce-scatter.7.cloned.1.call-update) | async-done | bytes 147472 | tf_op jit(solution)/shard_map/reduce_scatter | solution.py:240
  2402.2 98.2 %reduce-scatter.11.cloned.1.call-done = bf16[384,768]{1,0:T(8,128)(2,1)} async-done(((bf16[3072,768]{1,0:T(8,128)(2,1)}), bf16[384,768]{1,0:T(8,128)(2,1)}) %reduce-scatter.11.cloned.1.call-update) | async-done | bytes 589840 | tf_op jit(solution)/shard_map/reduce_scatter | solution.py:258
  2500.3 99.0 %reduce-scatter.9.cloned.1.call-done = bf16[96,3072]{1,0:T(8,128)(2,1)} async-done(((bf16[768,3072]{1,0:T(8,128)(2,1)}), bf16[96,3072]{1,0:T(8,128)(2,1)}) %reduce-scatter.9.cloned.1.call-update) | async-done | bytes 589840 | tf_op jit(solution)/shard_map/reduce_scatter | solution.py:252
  2599.3 82.6 %reduce-scatter.5.cloned.1.call-done = bf16[96,2304]{1,0:T(8,128)(2,1)} async-done(((bf16[768,2304]{1,0:T(8,128)(2,1)}), bf16[96,2304]{1,0:T(8,128)(2,1)}) %reduce-scatter.5.cloned.1.call-update) | async-done | bytes 442384 | tf_op jit(solution)/shard_map/reduce_scatter | solution.py:234
  2681.9 3.7 fusion.46
  2685.6 37.1 %all-reduce.8 = (bf16[768]{0:T(1024)(128)(2,1)}, bf16[768]{0:T(1024)(128)(2,1)}, bf16[2304]{0:T(1024)(128)(2,1)}, bf16[768]{0:T(1024)(128)(2,1)}, bf16[768]{0:T(...) all-reduce(bf16[768]{0:T(1024)(128)(2,1)} %get-tuple-element.17, ...), channel_id=3, replica_groups=mesh['batch'=4,'blk'=8] {'blk'}, use_global_device_ids=true, to_apply=%region_14.15.clone | all-reduce | flops 9984 | bytes 39936
  2732.9 6.4 all-reduce.9
  2749.5 5.4 add_convert_fusion.1
  (172 shorter events, 66.6 us)
Async XLA Ops:
  7.2 5.4 copy-start
  7.2 4.6 copy-start.27
  7.2 4.6 copy-start.33
  7.2 1931.1 %all-gather.3.cloned.1.call-start = ((), (), s32[]{:S(2)}) async-start(), calls=%async_computation.9 | async-start | bytes 113246208 | tf_op jit(solution)/shard_map/all_gather | solution.py:52
  7.3 4.6 copy-start.2
  7.3 5.3 copy-start.37
  9.1 3.4 copy-start.23
  12.5 4.1 copy-start.15
  16.6 2.1 copy-start.14
  16.6 3.8 copy-start.22
  18.8 1.6 copy-start.7
  39.4 2295.2 %all-reduce.14.cloned.1.call-start = ((), (), s32[]{:S(2)}) async-start(), calls=%async_computation.4 | async-start | bytes 12582912 | tf_op jit(solution)/shard_map/psum | solution.py:126
  42.2 5.6 copy-start.41
  1993.6 5.3 copy-start.1
  1993.6 5.3 copy-start.12
  2006.8 1.5 copy-start.17
  2006.8 2.0 copy-start.3
  2008.8 3.0 slice-start.7
  2009.2 2.6 slice-start.8
  2010.1 9.7 slice-start.5
  2011.7 8.1 slice-start.6
  2011.8 8.1 copy-start.38
  2011.8 8.0 copy-start.40
  2019.8 11.0 copy-start.11
  2063.8 3.6 copy-start.30
  2063.8 4.7 copy-start.36
  2073.7 9.3 slice-start
  2075.7 7.3 slice-start.1
  2075.7 8.3 slice-start.2
  2075.7 8.3 copy-start.20
  2098.4 10.4 copy-start.10
  2108.9 3.5 copy-start.5
  2123.2 279.0 %reduce-scatter.7.cloned.1.call-start = ((), (), s32[]{:S(2)}) async-start(), calls=%async_computation.6 | async-start | bytes 1327104 | tf_op jit(solution)/shard_map/reduce_scatter | solution.py:240
  2127.5 372.8 %reduce-scatter.11.cloned.1.call-start = ((), (), s32[]{:S(2)}) async-start(), calls=%async_computation.8 | async-start | bytes 5308416 | tf_op jit(solution)/shard_map/reduce_scatter | solution.py:258
  2140.9 458.4 %reduce-scatter.9.cloned.1.call-start = ((), (), s32[]{:S(2)}) async-start(), calls=%async_computation.7 | async-start | bytes 5308416 | tf_op jit(solution)/shard_map/reduce_scatter | solution.py:252
  2150.2 531.7 %reduce-scatter.5.cloned.1.call-start = ((), (), s32[]{:S(2)}) async-start(), calls=%async_computation.5 | async-start | bytes 3981312 | tf_op jit(solution)/shard_map/reduce_scatter | solution.py:234
  2334.5 5.7 copy-start.13
  2334.6 5.7 copy-start.16
  2338.6 1.6 copy-start.9
  2345.6 409.3 %all-reduce.16.cloned.1.call-start = ((), (), s32[]{:S(2)}) async-start(), calls=%async_computation.10 | async-start | bytes 3670016 | tf_op jit(solution)/shard_map/psum | solution.py:268
  2348.7 6.5 copy-start.4
  2348.7 6.5 copy-start.24
  2348.8 6.5 copy-start.28
  2355.2 3.1 copy-start.6
  2355.2 3.4 slice-start.3
  2356.1 3.3 slice-start.4
  2356.1 4.2 copy-start.8
  2754.9 7.4 copy-start.21
  (11 other events, 10.2 us)
Sparse Core Ops, SparseCore 0:
  39.5 1898.7 all-gather.2
  2123.3 211.2 all-reduce.13
  2338.9 63.2 reduce-scatter.6
  2406.1 94.2 reduce-scatter.10
  2504.3 94.9 reduce-scatter.8
  2603.2 78.6 reduce-scatter.4
  2685.4 47.4 all-reduce.15
